TPU v7x, 32 devices: a whole 2x2x4 slice. The times are simulated.
32 devices in a mesh: row: 4 (over z), col: 8 (over y, x, core).
Axes of the slice: x: 2, y: 2, z: 4, core: 2. Of those that a mesh axis runs over, the one named last changes fastest.
Arguments:
- kernel: bfloat16 [16384, 16384], P('row', 'col'), may hold values from -6 to 6
- labels: int32 [3, 16384], replicated, may hold values from 0 to 63, as said below
Outputs:
- distance: float32 [3, 16384, 64], P(None, ('row', 'col'))
- objective: float32 [3], replicated
Inputs may be any that keep to these rules, and one draw needn't show every extreme that they name: `labels`: in every iteration every cluster of 0 to 63 is named by at least one series.
All inputs are finite; a program needn't handle non-finite values.
Results may differ from a plain program's by a relative error of at most 0.0003.
Values sent between devices are 32-bit elements; how exact they have to be, the bound alone decides.
A program may use at most 64 MiB of HBM per device.

v0:
```python
import jax
import jax.numpy as jnp
from jax import lax
from jax.sharding import PartitionSpec as P

SERIES = 16384
CLUSTERS = 64
ITERS = 3


def shards(kernel, labels):
    rows_block, cols_block = kernel.shape
    slice_rows = rows_block // lax.axis_size("col")
    row_base = lax.axis_index("row") * rows_block
    col_base = lax.axis_index("col") * cols_block
    my_offset = lax.axis_index("col") * slice_rows
    clusters = jnp.arange(CLUSTERS, dtype=jnp.int32)
    col_labels = lax.dynamic_slice_in_dim(labels, col_base, cols_block, 1)
    block_labels = lax.dynamic_slice_in_dim(labels, row_base, rows_block, 1)
    counts = jnp.sum((labels[:, :, None] == clusters).astype(jnp.float32), axis=1)

    def encode(chosen):
        flat = chosen.T[:, :, None] == clusters[None, None, :]
        return flat.reshape(chosen.shape[1], -1).astype(jnp.bfloat16)

    local = jnp.dot(kernel, encode(col_labels), preferred_element_type=jnp.float32)
    whole = lax.psum(local, "col")
    totals = lax.psum(jnp.sum(encode(block_labels).astype(jnp.float32) * whole, axis=0), "row")
    sums = lax.dynamic_slice_in_dim(whole, my_offset, slice_rows, 0)
    sums, totals = (sums, totals)
    sums = sums.reshape(slice_rows, ITERS, CLUSTERS).transpose(1, 0, 2)
    totals = totals.reshape(ITERS, CLUSTERS)
    distance = -2.0 * sums / counts[:, None, :] + totals[:, None, :] / (counts * counts)[:, None, :]
    objective = 1.0 - jnp.sum(totals / counts, axis=1) / SERIES
    return (distance, objective)


def solution(mesh):
    return jax.shard_map(
        shards,
        mesh=mesh,
        in_specs=(P("row", "col"), P()),
        out_specs=(P(None, ("row", "col"), None), P()),
        check_vma=False,
    )
```

profile of v0, /device:TPU:0, one launch (start us, length us, event | category | flops | bytes accessed | tf_op | source)
XLA Modules:
  0.0 117.1 jit_solution(2459755366757021118)
XLA Ops:
  7.2 0.0 all-reduce.2.cloned.1.call-start
  7.2 0.1 eq.56
  7.3 0.8 dynamic-slice_bitcast_fusion.1
  8.1 0.3 bitcast_compare_fusion.1
  8.4 13.0 %convolution_bitcast_fusion = f32[4096,192]{0,1:T(8,128)} fusion(pred[2048,192]{0,1:T(32,128)(4,1)S(1)} %bitcast_compare_fusion.1, bf16[4096,2048]{1,0:T(8,128)(2,1)} %param.2), kind=kOutput, calls=%fused_computation.2 | convolution fusion | flops 3221225472 | bytes 20316160 | tf_op jit(solution)/shard_map/dot_general | solution.py:26
  21.4 0.0 copy-start
  21.4 0.0 all-reduce.2.cloned.1.call-update
  21.4 0.9 copy-done
  22.4 0.5 bitcast_compare_fusion
  22.9 2.0 %convert_reduce_fusion = f32[3,64]{1,0:T(4,128)S(1)} fusion(s32[3,16384]{1,0:T(4,128)S(1)} %copy-done), kind=kLoop, calls=%fused_computation | loop fusion | flops 9436992 | bytes 197376 | tf_op jit(solution)/shard_map/reduce_sum | solution.py:20
  24.9 68.7 %all-reduce.2.cloned.1.call-done = f32[4096,192]{0,1:T(8,128)} async-done(((f32[4096,192]{0,1:T(8,128)}), f32[4096,192]{0,1:T(8,128)}) %all-reduce.2.cloned.1.call-update) | async-done | bytes 3145744 | tf_op jit(solution)/shard_map/psum | solution.py:27
  93.6 2.4 %multiply_reduce_fusion = f32[192]{0:T(256)S(1)} fusion(f32[4096,192]{0,1:T(8,128)} %all-reduce.2.cloned.1.call-done, pred[4096,192]{0,1:T(8,128)(4,1)S(1)} %bitcast_compare_fusion), kind=kLoop, calls=%fused_computation.4 | loop fusion | flops 3145536 | bytes 3932928 | tf_op jit(solution)/shard_map/reduce_sum | solution.py:28
  96.0 0.1 broadcast_in_dim_reshape.3
  96.1 11.7 %psum.15 = f32[3,64]{1,0:T(4,128)S(1)} all-reduce(f32[3,64]{1,0:T(4,128)S(1)} %broadcast_in_dim_reshape.3), channel_id=1, replica_groups=mesh['row'=4,'col'=8] {'row'}, use_global_device_ids=true, to_apply=%region_3.0 | all-reduce | flops 192 | bytes 1536 | tf_op jit(solution)/shard_map/psum | solution.py:28
  107.8 0.1 divide_reduce_fusion
  107.9 0.5 multiply_subtract_fusion
  108.4 1.0 dynamic-slice_multiply_fusion
  109.4 0.9 add_bitcast_fusion
  (2 shorter events, 0.0 us)
Async XLA Ops:
  7.2 86.4 %all-reduce.2.cloned.1.call-start = ((), (), s32[]{:S(2)}) async-start(), calls=%async_computation | async-start | bytes 6291456 | tf_op jit(solution)/shard_map/psum | solution.py:27
  21.4 0.9 copy-start
Sparse Core Ops, SparseCore 0:
  21.6 71.9 all-reduce.1
where the time goes:
time: 117 us
  waiting for transfers between devices  68.8 us (59%)
  between operations  14.1 us (12%)
  matrix products  13 us (11%)
  blocking collectives  11.7 us (10%)
  other arithmetic  7.7 us (7%)
  local copies, waits for them, and re-layouts  1.86 us (2%)
    psum x1, waiting for transfers between devices, shards(): whole = lax.psum(local, 'col')  68.7 us
    dot_general x1, matrix products, shards(): jnp.dot(kernel, encode(col_labels), preferred_element_type=jnp.float32)  13 us
    psum x1, blocking collectives, shards(): lax.psum(jnp.sum(encode(block_labels).astype(jnp.float32) * whole, axis=0...  11.7 us
    reduce_sum x1, other arithmetic, shards(): jnp.sum(encode(block_labels).astype(jnp.float32) * whole, axis=0)  2.41 us
  transfers between devices with their start and end apart: 1, of which 1 were waited for; matrix products, arithmetic and copies ran while one was open for 2% of the time, Pallas kernels for 0%

commit v1 on v0

--- a/solution.py
+++ b/solution.py
@@ -24,7 +24,7 @@
         return flat.reshape(chosen.shape[1], -1).astype(jnp.bfloat16)
 
     local = jnp.dot(kernel, encode(col_labels), preferred_element_type=jnp.float32)
-    whole = lax.psum(local, "col")
+    whole = jnp.sum(lax.all_gather(local, "col"), axis=0)
     totals = lax.psum(jnp.sum(encode(block_labels).astype(jnp.float32) * whole, axis=0), "row")
     sums = lax.dynamic_slice_in_dim(whole, my_offset, slice_rows, 0)
     sums, totals = (sums, totals)

time: 117 us -> 201 us (1.72)
  waiting for transfers between devices: 68.8 us -> 124 us
  local copies, waits for them, and re-layouts: 1.86 us -> 24 us
  other arithmetic: 7.7 us -> 13.7 us
    all_gather x0 -> x1, waiting for transfers between devices: none -> 124 us  [shards(): whole = jnp.sum(lax.all_gather(local, 'col'), axis=0)]
    psum x1 -> x0, waiting for transfers between devices: 68.7 us -> none  [shards(): whole = lax.psum(local, 'col')]
    unnamed x2 -> x5, local copies, waits for them, and re-layouts: 0.92 us -> 23 us
    reduce_sum x0 -> x1, other arithmetic: none -> 8.03 us  [shards(): whole = jnp.sum(lax.all_gather(local, 'col'), axis=0)]
where the time goes in v1:
time: 201 us; the launch traced here: 200 us
  waiting for transfers between devices  124 us (62%)
  local copies, waits for them, and re-layouts  24 us (12%)
  between operations  14.1 us (7%)
  other arithmetic  13.7 us (7%)
  matrix products  13.1 us (7%)
  blocking collectives  11.7 us (6%)
    all_gather x1, waiting for transfers between devices, shards(): whole = jnp.sum(lax.all_gather(local, 'col'), axis=0)  124 us
    unnamed x5, local copies, waits for them, and re-layouts  23 us
    dot_general x1, matrix products, shards(): jnp.dot(kernel, encode(col_labels), preferred_element_type=jnp.float32)  13.1 us
    psum x1, blocking collectives, shards(): lax.psum(jnp.sum(encode(block_labels).astype(jnp.float32) * whole, axis=0...  11.7 us
    reduce_sum x1, other arithmetic, shards(): whole = jnp.sum(lax.all_gather(local, 'col'), axis=0)  8.03 us
  transfers between devices with their start and end apart: 1, of which 1 were waited for; matrix products, arithmetic and copies ran while one was open for 2% of the time, Pallas kernels for 0%

profile of v1, /device:TPU:0, one launch (start us, length us, event | category | flops | bytes accessed | tf_op | source)
XLA Modules:
  0.0 200.4 jit_solution(3998208494189982560)
XLA Ops:
  7.2 0.0 all-gather.3.cloned.1.call-start
  7.2 0.1 eq.60
  7.3 0.8 dynamic-slice_bitcast_fusion.1
  8.1 0.3 bitcast_compare_fusion.1
  8.4 13.1 %convolution_bitcast_fusion = f32[4096,192]{0,1:T(8,128)} fusion(pred[2048,192]{0,1:T(32,128)(4,1)S(1)} %bitcast_compare_fusion.1, bf16[4096,2048]{1,0:T(8,128)(2,1)} %param.2), kind=kOutput, calls=%fused_computation.3 | convolution fusion | flops 3221225472 | bytes 20316160 | tf_op jit(solution)/shard_map/dot_general | solution.py:26
  21.5 0.0 copy-start.1
  21.5 0.0 all-gather.3.cloned.1.call-update
  21.5 0.9 copy-done.1
  22.4 1.4 bitcast_compare_fusion
  23.8 2.0 convert_reduce_fusion
  25.8 123.8 %all-gather.3.cloned.1.call-done = f32[32768,192]{0,1:T(8,128)} async-done(((f32[4096,192]{0,1:T(8,128)}), f32[32768,192]{0,1:T(8,128)}) %all-gather.3.cloned.1.call-update) | async-done | bytes 25165840 | tf_op jit(solution)/shard_map/all_gather | solution.py:27
  149.6 22.1 %copy.5 = f32[24,8,8,4096]{3,2,1,0:T(8,128)S(1)} copy(f32[24,8,8,4096]{3,1,2,0:T(8,128)} %bitcast.20) | data formatting | bytes 50331648
  171.7 0.0 copy-start
  171.7 8.0 %bitcast_reduce_fusion = f32[4096,192]{0,1:T(8,128)S(1)} fusion(f32[24,8,8,4096]{3,2,1,0:T(8,128)S(1)} %copy.5), kind=kLoop, calls=%fused_computation | loop fusion | flops 5505024 | bytes 28311552 | tf_op jit(solution)/shard_map/reduce_sum | solution.py:27
  179.7 0.0 copy-done
  179.8 0.5 multiply_reduce_fusion
  180.3 0.1 broadcast_in_dim_reshape.3
  180.4 11.7 %psum.7 = f32[3,64]{1,0:T(4,128)S(1)} all-reduce(f32[3,64]{1,0:T(4,128)S(1)} %broadcast_in_dim_reshape.3), channel_id=1, replica_groups=mesh['row'=4,'col'=8] {'row'}, use_global_device_ids=true, to_apply=%region_3.0 | all-reduce | flops 192 | bytes 1536 | tf_op jit(solution)/shard_map/psum | solution.py:28
  192.1 0.1 divide_reduce_fusion
  192.2 0.5 multiply_subtract_fusion
  192.7 0.9 add_bitcast_fusion
  (3 shorter events, 0.0 us)
Async XLA Ops:
  7.2 142.4 %all-gather.3.cloned.1.call-start = ((), (), s32[]{:S(2)}) async-start(), calls=%async_computation | async-start | bytes 28311552 | tf_op jit(solution)/shard_map/all_gather | solution.py:27
  21.5 0.9 copy-start.1
  171.7 8.1 %copy-start = (pred[4096,192]{0,1:T(8,128)(4,1)S(1)}, pred[4096,192]{0,1:T(8,128)(4,1)}, u32[]{:S(2)}) copy-start(pred[4096,192]{0,1:T(8,128)(4,1)} %bitcast_compare_fusion) | copy-start | bytes 2359300
Sparse Core Ops, SparseCore 0:
  21.6 127.9 all-gather.2
